TPU v7x, 32 devices: a whole 2x2x4 slice. The times are simulated.
32 devices in a mesh: trial: 16 (over z, y, x), factor: 2 (over core).
Axes of the slice: x: 2, y: 2, z: 4, core: 2. Of those that a mesh axis runs over, the one named last changes fastest.
Arguments:
- observed: float32 [64, 32, 128], P('trial'), may hold values from -6 to 6
- trial_mean: float32 [64], P('trial'), may hold values from -4 to 4
- correlations: float32 [64, 2], P('trial'), may hold values from 0.1 to 0.7
- noise_var: float32 [64], P('trial'), may hold values from 2 to 8
- plot_slot: int32 [64, 32, 128], P('trial'), may hold values from 0 to 2047
- row_count: int32 [64], P('trial'), may hold values from 8 to 32, as said below
- col_count: int32 [64], P('trial'), may hold values from 64 to 128, as said below
- panel_list: int32 [64, 16], P('trial'), may hold values from 0 to 191, as said below
- scores: bfloat16 [128, 24576], P('factor', 'trial'), may hold values from -0.5 to 0.5
- loadings: float32 [64, 128], P('trial', 'factor'), may hold values from -5 to 5
- score_precision: float32 [128], P('factor'), may hold values from 20 to 80
Outputs:
- score_gradient: float32 [128, 24576], P('factor', 'trial')
- loading_gradient: float32 [64, 128], P('trial', 'factor')
Inputs may be any that keep to these rules, and one draw needn't show every extreme that they name: `panel_list`: panel p is owned by index p // 12 of trial. Among the 64 entries of each aligned block of 4 trials, no owner holds more than 8 of them, and in every block some owner holds exactly that many. Entries may repeat. `row_count`: the first trial uses all 32 rows. `col_count`: the first trial uses all 128 columns.
All inputs are finite; a program needn't handle non-finite values.
Results may differ from a plain program's by a relative error of at most 0.0023.
Values may be sent and summed in bfloat16 or wider, within the bound.
A program may use at most 64 MiB of HBM per device.

v0:
```python
import jax
import jax.numpy as jnp
from jax import lax
from jax.sharding import PartitionSpec as P

PANEL = 128


score_step = 0.005
load_step = 0.02


def sweep_axis(values_in, corr_value, position, limit_count, axis_number):
    factor_scale = 1.0 / (1.0 - corr_value * corr_value)
    interior = ((position > 0) & (position < limit_count - 1)).astype(values_in.dtype)
    padding = [(0, 0)] * values_in.ndim
    padding[axis_number] = (1, 1)
    padded = jnp.pad(values_in, padding)
    length = values_in.shape[axis_number]
    lower_side = lax.slice_in_dim(padded, 0, length, axis=axis_number)
    upper_side = lax.slice_in_dim(padded, 2, length + 2, axis=axis_number)
    result = factor_scale * (
        (1.0 + corr_value * corr_value * interior) * values_in
        - corr_value * (lower_side + upper_side)
    )
    return jnp.where(position < limit_count, result, 0.0)


def body(
    observed,
    trial_mean,
    correlations,
    noise_var,
    plot_slot,
    row_count,
    col_count,
    panel_list,
    scores,
    loadings,
    score_precision,
):
    trial_count = lax.axis_size("trial")
    per_dev = panel_list.shape[0]
    per_trial = panel_list.shape[1]
    required_count = per_dev * per_trial
    most_count = 2 * required_count // trial_count
    slots_total = trial_count * most_count
    latent_factor_count = scores.shape[0]
    owned_panels = scores.shape[1] // PANEL
    slots_trial = per_trial * PANEL
    wanted = panel_list.reshape(required_count)
    owner_of = wanted // owned_panels
    local_of = wanted - owner_of * owned_panels
    later_pos = lax.broadcasted_iota(jnp.int32, (required_count, required_count), 0)
    other_pos = lax.broadcasted_iota(jnp.int32, (required_count, required_count), 1)
    earlier = (owner_of[None, :] == owner_of[:, None]) & (other_pos < later_pos)
    rank_of = jnp.sum(earlier.astype(jnp.int32), axis=1)
    position = owner_of * most_count + rank_of
    placer_int = (
        position[None, :] == lax.broadcasted_iota(jnp.int32, (slots_total, required_count), 0)
    ).astype(jnp.int32)
    request = jnp.sum(placer_int * (local_of[None, :] + 1), axis=1) - 1
    placer = placer_int.astype(jnp.float32)
    incoming = lax.all_to_all(request, "trial", split_axis=0, concat_axis=0, tiled=True)
    picker = (
        incoming[None, :] == lax.broadcasted_iota(jnp.int32, (owned_panels, slots_total), 0)
    ).astype(jnp.float32)
    grid_shape = observed.shape
    plot_count = grid_shape[1] * grid_shape[2]
    row_index = lax.broadcasted_iota(jnp.int32, grid_shape, 1)
    col_index = lax.broadcasted_iota(jnp.int32, grid_shape, 2)
    row_upper_limit = row_count[:, None, None]
    col_limit = col_count[:, None, None]
    active = (row_index < row_upper_limit) & (col_index < col_limit)
    flat_slot = plot_slot.reshape(per_dev, plot_count)
    panel_of_plot = flat_slot // PANEL
    cell_of_plot = flat_slot - panel_of_plot * PANEL
    panel_onehot_matrix = (
        panel_of_plot[:, :, None]
        == lax.broadcasted_iota(jnp.int32, (per_dev, plot_count, per_trial), 2)
    ).astype(jnp.float32)
    cell_match = cell_of_plot[:, :, None] == lax.broadcasted_iota(
        jnp.int32, (per_dev, plot_count, PANEL), 2
    )
    correlation_row_values = correlations[:, 0][:, None, None]
    corr_cols = correlations[:, 1][:, None, None]

    def fetch(current):
        whole = lax.all_gather(current, "trial", axis=1, tiled=True)
        grouped = whole.reshape(latent_factor_count, -1, PANEL)
        panel_total = grouped.shape[1]
        chooser = (
            wanted[None, :] == lax.broadcasted_iota(jnp.int32, (panel_total, required_count), 0)
        ).astype(jnp.bfloat16)
        picked = jnp.einsum(
            "kqc,qn->knc", grouped, chooser, preferred_element_type=jnp.float32
        ).astype(jnp.bfloat16)
        return picked.reshape(latent_factor_count, per_dev, slots_trial)

    def evaluate(current, loads_now):
        table = fetch(current)
        table_wide = table.astype(jnp.float32)
        partial_effect = jnp.einsum(
            "ktn,tk->tn", table_wide, loads_now, precision=lax.Precision.HIGHEST
        )
        effect = lax.psum(partial_effect, "factor")
        effect_table_grid = effect.reshape(per_dev, per_trial, PANEL)
        rows_picked = jnp.einsum(
            "jwo,jom->jwm", panel_onehot_matrix, effect_table_grid, precision=lax.Precision.HIGHEST
        )
        fitted = jnp.sum(jnp.where(cell_match, rows_picked, 0.0), axis=2).reshape(grid_shape)
        residual = jnp.where(active, observed - trial_mean[:, None, None] - fitted, 0.0)
        across = sweep_axis(residual, corr_cols, col_index, col_limit, 2)
        weighted = (
            sweep_axis(across, correlation_row_values, row_index, row_upper_limit, 1)
            / noise_var[:, None, None]
        )
        dispersion_amount = jnp.where(
            cell_match, weighted.reshape(per_dev, plot_count)[:, :, None], 0.0
        )
        slot_weight = jnp.einsum(
            "boy,bom->bym", panel_onehot_matrix, dispersion_amount, precision=lax.Precision.HIGHEST
        ).reshape(per_dev, slots_trial)
        load_grad = -jnp.einsum(
            "ktn,tn->tk", table_wide, slot_weight, precision=lax.Precision.HIGHEST
        )
        returned = -(loads_now.T[:, :, None] * slot_weight[None, :, :])
        returned = returned.reshape(latent_factor_count, required_count, PANEL)
        outgoing = jnp.einsum("jn,knc->kjc", placer, returned, precision=lax.Precision.HIGHEST)
        arrived = lax.all_to_all(outgoing, "trial", split_axis=1, concat_axis=1, tiled=True)
        summed = jnp.einsum("qj,kjc->kqc", picker, arrived, precision=lax.Precision.HIGHEST)
        score_grad = score_precision[:, None] * current.astype(jnp.float32) + summed.reshape(
            latent_factor_count, owned_panels * PANEL
        )
        return (score_grad, load_grad)

    first_scores, first_loads = evaluate(scores, loadings)
    new_scores = (scores.astype(jnp.float32) - score_step * first_scores).astype(jnp.bfloat16)
    new_loads = loadings - load_step * first_loads
    return evaluate(new_scores, new_loads)


def solution(mesh):
    in_specs = (
        P("trial", None, None),
        P("trial"),
        P("trial", None),
        P("trial"),
        P("trial", None, None),
        P("trial"),
        P("trial"),
        P("trial", None),
        P("factor", "trial"),
        P("trial", "factor"),
        P("factor"),
    )
    out_specs = (P("factor", "trial"), P("trial", "factor"))
    return jax.shard_map(body, mesh=mesh, in_specs=in_specs, out_specs=out_specs, check_vma=False)
```

profile of v0, /device:TPU:14, one launch (start us, length us, event | category | flops | bytes accessed | tf_op | source)
XLA Modules:
  0.0 437.5 jit_solution(3423635285913149859)
XLA Ops:
  7.9 0.8 eq.65
  9.7 7.1 %all-to-all-start.1 = ((s32[16,8,1]{1,2,0:T(1,128)}), s32[16,8,1]{1,2,0:T(1,128)S(1)}, u32[]{:S(2)}, u32[]{:S(2)}) async-start(s32[16,8,1]{1,2,0:T(1,128)} %bitcast.12), calls=%async_computation.1 | async-start | bytes 16384 | tf_op jit(solution)/shard_map/all_to_all | solution.py:64
  18.9 0.8 slice_bitcast_fusion.1
  19.7 0.8 subtract_divide_fusion.1
  20.4 0.9 bitcast_subtract_fusion.2
  21.4 57.7 %all-gather.3.cloned.1.call-done = bf16[64,24576]{1,0:T(8,128)(2,1)} async-done(((bf16[64,1536]{1,0:T(8,128)(2,1)}), bf16[64,24576]{1,0:T(8,128)(2,1)}) %all-gather.3.cloned.1.call-update) | async-done | bytes 3145744 | tf_op jit(solution)/shard_map/all_gather | solution.py:89
  79.1 2.7 copy.52
  82.8 1.5 fusion.30
  84.4 3.9 psum.14
  88.4 4.5 %select_reduce_fusion.1 = f32[4,4096]{1,0:T(4,128)S(1)} fusion(f32[4,16,128]{2,1,0:T(8,128)S(1)} %psum.14, s32[4,4096]{1,0:T(4,128)S(1)} %get-tuple-element.4, s32[4,4096]{1,0:T(4,128)S(1)} %get-tuple-element.5), kind=kOutput, calls=%fused_computation.5 | convolution fusion | flops 409190400 | bytes 229376 | tf_op jit(solution)/shard_map/jwo,jom->jwm/dot_general | solution.py:108
  93.3 4.7 %fusion.2 = f32[4,16,128]{2,1,0:T(8,128)S(1)} fusion(f32[4,4096]{1,0:T(4,128)S(1)} %bitcast.142, s32[4,4096]{1,0:T(4,128)S(1)} %get-tuple-element.4, s32[4,4096]{1,0:T(4,128)S(1)} %get-tuple-element.5), kind=kOutput, calls=%fused_computation.3 | convolution fusion | flops 407109632 | bytes 229376 | tf_op jit(solution)/shard_map/boy,bom->bym/dot_general | solution.py:121
  98.0 8.8 %convolution_bitcast_fusion.1 = f32[64,128,128]{1,2,0:T(8,128)} fusion(f32[64,128]{1,0:T(8,128)S(1)} %bitcast.143, f32[64,64]{1,0:T(8,128)S(1)} %copy.30, s32[64]{0:T(128)S(1)} %multiply_add_fusion), kind=kOutput, calls=%fused_computation.18 | convolution fusion | flops 806379520 | bytes 4243712 | tf_op jit(solution)/shard_map/jn,knc->kjc/dot_general | solution.py:129
  106.9 5.4 %copy.32 = f32[64,128,128]{2,0,1:T(8,128)} copy(f32[64,128,128]{1,2,0:T(8,128)} %convolution_bitcast_fusion.1) | data formatting | bytes 8388608 | tf_op jit(solution)/shard_map/jn,knc->kjc/transpose | solution.py:129
  112.3 5.7 %all-to-all-start = ((f32[64,128,128]{2,0,1:T(8,128)}), f32[64,128,128]{2,0,1:T(8,128)}, u32[]{:S(2)}, u32[]{:S(2)}) async-start(f32[64,128,128]{2,0,1:T(8,128)} %copy.32), calls=%async_computation | async-start | bytes 8388608 | tf_op jit(solution)/shard_map/all_to_all | solution.py:130
  119.6 95.1 %all-to-all-done = f32[64,128,128]{2,0,1:T(8,128)} async-done(((f32[64,128,128]{2,0,1:T(8,128)}), f32[64,128,128]{2,0,1:T(8,128)}, u32[]{:S(2)}, u32[]{:S(2)}) %all-to-all-start) | async-done | bytes 4194336 | tf_op jit(solution)/shard_map/all_to_all | solution.py:130
  214.6 5.8 %fusion.6 = f32[64,128,12]{1,2,0:T(8,128)S(1)} fusion(f32[64,128,128]{2,0,1:T(8,128)} %all-to-all-done, s32[128]{0:T(128)S(1)} %eq.73), kind=kOutput, calls=%fused_computation.9 | convolution fusion | flops 150996480 | bytes 4588032 | tf_op jit(solution)/shard_map/qj,kjc->kqc/dot_general | solution.py:131
  220.4 0.9 fusion.38
  221.4 1.3 fusion.28
  222.7 65.6 %all-gather.5.cloned.1.call-done = bf16[64,24576]{1,0:T(8,128)(2,1)} async-done(((bf16[64,1536]{1,0:T(8,128)(2,1)}), bf16[64,24576]{1,0:T(8,128)(2,1)}) %all-gather.5.cloned.1.call-update) | async-done | bytes 3145744 | tf_op jit(solution)/shard_map/all_gather | solution.py:89
  288.4 2.7 copy.57
  291.1 0.7 fusion.19
  292.1 1.5 fusion.26
  293.7 3.6 psum.15
  297.3 4.5 %select_reduce_fusion = f32[4,4096]{1,0:T(4,128)S(1)} fusion(f32[4,16,128]{2,1,0:T(8,128)S(1)} %psum.15, s32[4,4096]{1,0:T(4,128)S(1)} %get-tuple-element.4, s32[4,4096]{1,0:T(4,128)S(1)} %get-tuple-element.5), kind=kOutput, calls=%fused_computation.2 | convolution fusion | flops 409190400 | bytes 229376 | tf_op jit(solution)/shard_map/jwo,jom->jwm/dot_general | solution.py:108
  302.2 4.7 %fusion = f32[4,16,128]{2,1,0:T(8,128)S(1)} fusion(f32[4,4096]{1,0:T(4,128)S(1)} %bitcast.141, s32[4,4096]{1,0:T(4,128)S(1)} %get-tuple-element.4, s32[4,4096]{1,0:T(4,128)S(1)} %get-tuple-element.5), kind=kOutput, calls=%fused_computation | convolution fusion | flops 407109632 | bytes 229376 | tf_op jit(solution)/shard_map/boy,bom->bym/dot_general | solution.py:121
  306.9 8.8 %convolution_bitcast_fusion = f32[64,128,128]{1,2,0:T(8,128)} fusion(f32[64,128]{1,0:T(8,128)S(1)} %bitcast.145, f32[64,64]{1,0:T(8,128)S(1)} %copy.35, s32[64]{0:T(128)S(1)} %multiply_add_fusion), kind=kOutput, calls=%fused_computation.17 | convolution fusion | flops 806379520 | bytes 4243712 | tf_op jit(solution)/shard_map/jn,knc->kjc/dot_general | solution.py:129
  315.7 5.4 %copy.37 = f32[64,128,128]{2,0,1:T(8,128)} copy(f32[64,128,128]{1,2,0:T(8,128)} %convolution_bitcast_fusion) | data formatting | bytes 8388608 | tf_op jit(solution)/shard_map/jn,knc->kjc/transpose | solution.py:129
  321.2 6.1 %all-to-all-start.2 = ((f32[64,128,128]{2,0,1:T(8,128)}), f32[64,128,128]{2,0,1:T(8,128)}, u32[]{:S(2)}, u32[]{:S(2)}) async-start(f32[64,128,128]{2,0,1:T(8,128)} %copy.37), calls=%async_computation.2 | async-start | bytes 8388608 | tf_op jit(solution)/shard_map/all_to_all | solution.py:130
  327.3 1.3 fusion.24
  329.2 94.4 %all-to-all-done.2 = f32[64,128,128]{2,0,1:T(8,128)} async-done(((f32[64,128,128]{2,0,1:T(8,128)}), f32[64,128,128]{2,0,1:T(8,128)}, u32[]{:S(2)}, u32[]{:S(2)}) %all-to-all-start.2) | async-done | bytes 4194336 | tf_op jit(solution)/shard_map/all_to_all | solution.py:130
  423.6 5.8 %fusion.4 = f32[64,128,12]{1,2,0:T(8,128)S(1)} fusion(f32[64,128,128]{2,0,1:T(8,128)} %all-to-all-done.2, s32[128]{0:T(128)S(1)} %eq.73), kind=kOutput, calls=%fused_computation.7 | convolution fusion | flops 150996480 | bytes 4588032 | tf_op jit(solution)/shard_map/qj,kjc->kqc/dot_general | solution.py:131
  429.4 0.9 bitcast_add_fusion
  (57 shorter events, 8.1 us)
Async XLA Ops:
  7.2 71.9 %all-gather.3.cloned.1.call-start = ((), (), s32[]{:S(2)}) async-start(), calls=%async_computation.3 | async-start | bytes 3342336 | tf_op jit(solution)/shard_map/all_gather | solution.py:89
  9.7 102.6 %all-to-all-start.1 = ((s32[16,8,1]{1,2,0:T(1,128)}), s32[16,8,1]{1,2,0:T(1,128)S(1)}, u32[]{:S(2)}, u32[]{:S(2)}) async-start(s32[16,8,1]{1,2,0:T(1,128)} %bitcast.12), calls=%async_computation.1 | async-start | bytes 16384 | tf_op jit(solution)/shard_map/all_to_all | solution.py:64
  81.8 1.0 copy-start.5
  88.3 4.5 %copy-start.2 = (f32[4,32,128]{2,1,0:T(8,128)S(1)}, f32[4,32,128]{2,1,0:T(8,128)}, u32[]{:S(2)}) copy-start(f32[4,32,128]{2,1,0:T(8,128)} %param.11) | copy-start | bytes 196612
  88.4 4.5 %copy-start.3 = (s32[4]{0:T(128)S(1)}, s32[4]{0:T(128)}, u32[]{:S(2)}) copy-start(s32[4]{0:T(128)} %param.17) | copy-start | bytes 52
  88.4 4.5 %copy-start.4 = (s32[4]{0:T(128)S(1)}, s32[4]{0:T(128)}, u32[]{:S(2)}) copy-start(s32[4]{0:T(128)} %param.16) | copy-start | bytes 52
  88.4 4.5 %copy-start.6 = (f32[4]{0:T(128)S(1)}, f32[4]{0:T(128)}, u32[]{:S(2)}) copy-start(f32[4]{0:T(128)} %param.12) | copy-start | bytes 52
  88.4 4.8 %copy-start.7 = (f32[4]{0:T(128)S(1)}, f32[4]{0:T(128)}, u32[]{:S(2)}) copy-start(f32[4]{0:T(128)} %param.14) | copy-start | bytes 52
  112.3 102.3 %all-to-all-start = ((f32[64,128,128]{2,0,1:T(8,128)}), f32[64,128,128]{2,0,1:T(8,128)}, u32[]{:S(2)}, u32[]{:S(2)}) async-start(f32[64,128,128]{2,0,1:T(8,128)} %copy.32), calls=%async_computation | async-start | bytes 8388608 | tf_op jit(solution)/shard_map/all_to_all | solution.py:130
  118.0 102.4 %copy-start.1 = (bf16[64,1536]{1,0:T(8,128)(2,1)S(1)}, bf16[64,1536]{1,0:T(8,128)(2,1)}, u32[]{:S(2)}) copy-start(bf16[64,1536]{1,0:T(8,128)(2,1)} %param.19) | copy-start | bytes 589828
  118.0 102.4 %copy-start.8 = (f32[64]{0:T(128)S(1)}, f32[64]{0:T(128)}, u32[]{:S(2)}) copy-start(f32[64]{0:T(128)} %param.21) | copy-start | bytes 772
  118.1 170.3 %all-gather.5.cloned.1.call-start = ((), (), s32[]{:S(2)}) async-start(), calls=%async_computation.4 | async-start | bytes 3342336 | tf_op jit(solution)/shard_map/all_gather | solution.py:89
  321.2 102.5 %all-to-all-start.2 = ((f32[64,128,128]{2,0,1:T(8,128)}), f32[64,128,128]{2,0,1:T(8,128)}, u32[]{:S(2)}, u32[]{:S(2)}) async-start(f32[64,128,128]{2,0,1:T(8,128)} %copy.37), calls=%async_computation.2 | async-start | bytes 8388608 | tf_op jit(solution)/shard_map/all_to_all | solution.py:130
  327.3 102.1 %copy-start = (bf16[64,1536]{1,0:T(8,128)(2,1)S(1)}, bf16[64,1536]{1,0:T(8,128)(2,1)}, u32[]{:S(2)}) copy-start(bf16[64,1536]{1,0:T(8,128)(2,1)} %fusion.38) | copy-start | bytes 589828
Sparse Core Ops, SparseCore 0:
  10.7 68.3 all-gather.2
  221.5 66.8 all-gather.4
where the time goes:
time: 441 us; the launch traced here: 437 us
  waiting for transfers between devices  314 us (71%)
  matrix products  54.7 us (12%)
  local copies, waits for them, and re-layouts  20.7 us (5%)
  starting transfers between devices  19.3 us (4%)
  between operations  14.7 us (3%)
  blocking collectives  7.55 us (2%)
  other arithmetic  7.07 us (2%)
    all_to_all x2, waiting for transfers between devices, evaluate(): lax.all_to_all(outgoing, 'trial', split_axis=1, concat_axis=1, tiled=True)  190 us
    all_gather x2, waiting for transfers between devices, fetch(): whole = lax.all_gather(current, 'trial', axis=1, tiled=True)  123 us
    dot_general x2, matrix products, evaluate(): jnp.einsum('jn,knc->kjc', placer, returned, precision=lax.Precision.HIGHEST)  17.7 us
    all_to_all x2, starting transfers between devices, evaluate(): lax.all_to_all(outgoing, 'trial', split_axis=1, concat_axis=1, tiled=True)  11.9 us
    dot_general x2, matrix products, evaluate(): jnp.einsum('qj,kjc->kqc', picker, arrived, precision=lax.Precision.HIGHEST)  11.6 us
    transpose x2, local copies, waits for them, and re-layouts, evaluate(): jnp.einsum('jn,knc->kjc', placer, returned, precision=lax.Precision.HIGHEST)  10.8 us
    dot_general x2, matrix products, evaluate(): jnp.einsum('boy,bom->bym', panel_onehot_matrix, dispersion_amount, precis...  9.44 us
    dot_general x2, matrix products, evaluate(): jnp.einsum('jwo,jom->jwm', panel_onehot_matrix, effect_table_grid, precis...  8.94 us
  transfers between devices with their start and end apart: 5, of which 4 were waited for; matrix products, arithmetic and copies ran while one was open for 9% of the time, Pallas kernels for 0%

commit v1 on v0

v1 whole, which is shorter than its diff:
```python
import functools

import jax
import jax.numpy as jnp
from jax import lax
from jax.experimental import pallas as pl
from jax.experimental.pallas import tpu as pltpu
from jax.sharding import PartitionSpec as P

PANEL = 128
TILE = 8

score_step = 0.005
load_step = 0.02

MESH = pl.DeviceIdType.MESH
F32 = jnp.float32
BF16 = jnp.bfloat16


def halves(x):
    high = x.astype(BF16).astype(F32)
    return high, x - high


def dot(a, b):
    return lax.dot_general(a, b, (((1,), (0,)), ((), ())), preferred_element_type=F32)


def dot_nt(a, b):
    return lax.dot_general(a, b, (((1,), (1,)), ((), ())), preferred_element_type=F32)


def kernel(
    n_trial,
    n_factor,
    rank_tile,
    mean_ref,
    corr_ref,
    noise_ref,
    rows_ref,
    cols_ref,
    observed_ref,
    slot_ref,
    scores_ref,
    loads_ref,
    precision_ref,
    source_ref,
    local_ref,
    place_ref,
    score_out,
    load_out,
    sent,
    got,
    fac_sent,
    fac_got,
    spread,
    cells,
    fresh,
    send_sem,
    recv_sem,
    fac_send_sem,
    fac_recv_sem,
):
    per_dev, grid_rows, grid_cols = observed_ref.shape
    factors = scores_ref.shape[0]
    owned = scores_ref.shape[1] // PANEL
    required = place_ref.shape[0]
    per_trial = required // per_dev
    rows = n_trial * rank_tile
    me = lax.axis_index("trial")
    mine = lax.axis_index("factor")

    barrier = pltpu.get_barrier_semaphore()
    for step in range(1, n_trial):
        pl.semaphore_signal(
            barrier,
            inc=1,
            device_id={"trial": lax.rem(me + step, n_trial)},
            device_id_type=MESH,
        )
    for step in range(1, n_factor):
        pl.semaphore_signal(
            barrier,
            inc=1,
            device_id={"factor": lax.rem(mine + step, n_factor)},
            device_id_type=MESH,
        )

    def tile_at(index):
        return pl.ds(pl.multiple_of(index * rank_tile, rank_tile), rank_tile)

    def send(number):
        got[number, tile_at(me), :] = sent[number, tile_at(me), :]
        for step in range(1, n_trial):
            target = lax.rem(me + step, n_trial)
            pltpu.make_async_remote_copy(
                src_ref=sent.at[number, tile_at(target)],
                dst_ref=got.at[number, tile_at(me)],
                send_sem=send_sem.at[number],
                recv_sem=recv_sem.at[number],
                device_id={"trial": target},
                device_id_type=MESH,
            ).start()

    def others(number, ref, sem):
        part = ref.at[number, pl.ds(0, (n_trial - 1) * rank_tile)]
        return pltpu.make_async_copy(part, part, sem.at[number])

    def receive(number):
        others(number, got, recv_sem).wait()
        return got[number]

    def factor_sum(number, part):
        fac_sent[number] = part
        fac_got[number, pl.ds(mine, 1)] = part[None]
        for step in range(1, n_factor):
            pltpu.make_async_remote_copy(
                src_ref=fac_sent.at[number],
                dst_ref=fac_got.at[number, mine],
                send_sem=fac_send_sem.at[number, step - 1],
                recv_sem=fac_recv_sem.at[number, step - 1],
                device_id={"factor": lax.rem(mine + step, n_factor)},
                device_id_type=MESH,
            ).start()
        for step in range(1, n_factor):
            origin = lax.rem(mine + n_factor - step, n_factor)
            pltpu.make_async_copy(
                fac_sent.at[number], fac_got.at[number, origin], fac_recv_sem.at[number, step - 1]
            ).wait()
        total = fac_got[number, 0]
        for index in range(1, n_factor):
            total = total + fac_got[number, index]
        return total

    source = source_ref[...]
    trial_of = jnp.where(source >= 0, source // per_trial, -1)
    local_of = local_ref[...]

    def load_rows(loads):
        total = jnp.zeros((rows, factors), F32)
        for trial in range(per_dev):
            total = jnp.where(trial_of == trial, loads[trial : trial + 1, :], total)
        return total

    loads = loads_ref[...]
    sent[0, :, :] = jnp.concatenate(
        [
            load_rows(loads),
            jnp.broadcast_to(local_of, (rows, PANEL - factors)),
        ],
        axis=1,
    )
    pl.semaphore_wait(barrier, n_trial - 1 + n_factor - 1)
    send(0)

    lane_rows = lax.broadcasted_iota(jnp.int32, (required, rows), 1)
    unpack = jnp.where(place_ref[...] == lane_rows, 1.0, 0.0).astype(BF16)
    unpack = jnp.concatenate([unpack, unpack], axis=1)
    lane_slots = lax.broadcasted_iota(jnp.int32, (rows, required), 1)
    pack = jnp.where(source == lane_slots, 1.0, 0.0)
    pack = jnp.concatenate([pack, pack], axis=1).astype(BF16)
    cell_iota = lax.broadcasted_iota(jnp.int32, (PANEL, grid_cols), 0)
    panel_iota = lax.broadcasted_iota(jnp.int32, (per_trial, grid_cols), 0)
    for trial in range(per_dev):
        cell = slot_ref[trial] & (PANEL - 1)
        for row in range(grid_rows):
            cells[trial, :, row * grid_cols : (row + 1) * grid_cols] = jnp.where(
                cell[row : row + 1, :] == cell_iota, 1.0, 0.0
            ).astype(BF16)

    row_index = lax.broadcasted_iota(jnp.int32, (grid_rows, grid_cols), 0)
    col_index = lax.broadcasted_iota(jnp.int32, (grid_rows, grid_cols), 1)

    def sweep(values, corr, position, limit, axis):
        length = values.shape[axis]
        scale = 1.0 / (1.0 - corr * corr)
        inner = jnp.where((position > 0) & (position < limit - 1), corr * corr, 0.0)
        lower = jnp.where(position == 0, 0.0, pltpu.roll(values, 1, axis))
        upper = jnp.where(position == length - 1, 0.0, pltpu.roll(values, length - 1, axis))
        result = scale * ((1.0 + inner) * values - corr * (lower + upper))
        return jnp.where(position < limit, result, 0.0)

    def plots(effect):
        totals = []
        for trial in range(per_dev):
            slot = slot_ref[trial]
            panel = slot // PANEL
            cell = slot & (PANEL - 1)
            fitted = jnp.zeros((grid_rows, grid_cols), F32)
            for index in range(per_trial):
                at = trial * per_trial + index
                line = jnp.broadcast_to(effect[at : at + 1, :], (grid_rows, PANEL))
                taken = jnp.take_along_axis(line, cell, axis=1)
                fitted = jnp.where(panel == index, taken, fitted)
            row_limit = rows_ref[trial]
            col_limit = cols_ref[trial]
            active = (row_index < row_limit) & (col_index < col_limit)
            residual = jnp.where(active, observed_ref[trial] - mean_ref[trial] - fitted, 0.0)
            row_corr = jnp.full((grid_rows, grid_cols), corr_ref[trial, 0], F32)
            col_corr = jnp.full((grid_rows, grid_cols), corr_ref[trial, 1], F32)
            noise = jnp.full((grid_rows, grid_cols), noise_ref[trial], F32)
            across = sweep(residual, col_corr, col_index, col_limit, 1)
            weighted = sweep(across, row_corr, row_index, row_limit, 0) / noise
            high, low = halves(weighted)
            for row in range(grid_rows):
                match = panel[row : row + 1, :] == panel_iota
                where_to = slice(row * grid_cols, (row + 1) * grid_cols)
                spread[trial, 0:per_trial, where_to] = jnp.where(
                    match, high[row : row + 1, :], 0.0
                ).astype(BF16)
                spread[trial, per_trial : 2 * per_trial, where_to] = jnp.where(
                    match, low[row : row + 1, :], 0.0
                ).astype(BF16)
            both = dot_nt(spread[trial], cells[trial])
            totals.append(both[0:per_trial] + both[per_trial : 2 * per_trial])
        return jnp.concatenate(totals, axis=0)

    def evaluate(first, load_part, panel_of, panel_lane, current_ref):
        load_high, load_low = halves(load_part)
        load_both = jnp.concatenate([load_high, load_low], axis=1).astype(BF16)
        effect = jnp.zeros((rows, PANEL), F32)
        for panel in range(owned):
            block = current_ref[:, panel * PANEL : (panel + 1) * PANEL]
            product = dot(load_both, jnp.concatenate([block, block], axis=0))
            effect = jnp.where(panel_of == panel, product, effect)
        sent[first] = effect
        send(first)
        arrived_high, arrived_low = halves(receive(first))
        table = dot(unpack, jnp.concatenate([arrived_high, arrived_low], axis=0).astype(BF16))
        slot_weight = plots(factor_sum(0 if first == 1 else 1, table))
        high, low = halves(slot_weight)
        sent[first + 1] = dot(pack, jnp.concatenate([high, low], axis=0).astype(BF16))
        send(first + 1)
        weight = receive(first + 1)
        high, low = halves(weight)
        weight_wide = jnp.concatenate([high, low], axis=1).astype(BF16)
        terms = jnp.zeros((rows, factors), F32)
        for panel in range(owned):
            block = current_ref[:, panel * PANEL : (panel + 1) * PANEL]
            product = dot_nt(weight_wide, jnp.concatenate([block, block], axis=1))
            terms = jnp.where(panel_of == panel, product, terms)
        sent[first + 2] = jnp.concatenate(
            [terms, jnp.zeros((rows, PANEL - factors), F32)], axis=1
        )
        send(first + 2)
        weight_tall = jnp.concatenate([high, low, high], axis=0).astype(BF16)
        lane_high, lane_low = halves(load_part_t(load_part))
        for panel in range(owned):
            where_to = slice(panel * PANEL, (panel + 1) * PANEL)
            match = panel_lane == panel
            masked_high = jnp.where(match, lane_high, 0.0)
            masked_low = jnp.where(match, lane_low, 0.0)
            left = jnp.concatenate([masked_high, masked_high, masked_low], axis=1).astype(BF16)
            current = current_ref[:, where_to].astype(F32)
            grad = precision_ref[...] * current - dot(left, weight_tall)
            if first == 1:
                fresh[:, where_to] = (current - score_step * grad).astype(BF16)
            else:
                score_out[:, where_to] = grad
        back = receive(first + 2)[:, 0:factors]
        sums = []
        for trial in range(per_dev):
            sums.append(
                jnp.sum(jnp.where(trial_of == trial, back, 0.0), axis=0, keepdims=True)
            )
        return jnp.concatenate(sums, axis=0)

    def load_part_t(load_part):
        wide = jnp.concatenate([load_part, jnp.zeros((rows, PANEL - factors), F32)], axis=1)
        return wide.T[0:factors, :]

    message = receive(0)
    panel_of = message[:, factors : factors + 1]
    panel_lane = message.T[factors : factors + 1, :]
    gained = evaluate(1, message[:, 0:factors], panel_of, panel_lane, scores_ref)
    new_loads = loads + load_step * gained
    sent[4] = jnp.concatenate(
        [load_rows(new_loads), jnp.zeros((rows, PANEL - factors), F32)], axis=1
    )
    send(4)
    gained = evaluate(5, receive(4)[:, 0:factors], panel_of, panel_lane, fresh)
    load_out[...] = -gained

    for number in range(8):
        others(number, sent, send_sem).wait()
    for number in range(2):
        for step in range(1, n_factor):
            pltpu.make_async_copy(
                fac_sent.at[number], fac_sent.at[number], fac_send_sem.at[number, step - 1]
            ).wait()


def body(
    observed,
    trial_mean,
    correlations,
    noise_var,
    plot_slot,
    row_count,
    col_count,
    panel_list,
    scores,
    loadings,
    score_precision,
):
    n_trial = lax.axis_size("trial")
    n_factor = lax.axis_size("factor")
    per_dev, per_trial = panel_list.shape
    required = per_dev * per_trial
    most = 2 * required // n_trial
    rank_tile = -(-most // TILE) * TILE
    rows = n_trial * rank_tile
    factors = scores.shape[0]
    owned = scores.shape[1] // PANEL
    wanted = panel_list.reshape(required)
    owner = wanted // owned
    local = wanted - owner * owned
    later = lax.broadcasted_iota(jnp.int32, (required, required), 0)
    other = lax.broadcasted_iota(jnp.int32, (required, required), 1)
    earlier = (owner[None, :] == owner[:, None]) & (other < later)
    place = owner * rank_tile + jnp.sum(earlier.astype(jnp.int32), axis=1)
    placed = place[None, :] == lax.broadcasted_iota(jnp.int32, (rows, required), 0)
    slots = lax.broadcasted_iota(jnp.int32, (rows, required), 1)
    source = jnp.max(jnp.where(placed, slots, -1), axis=1, keepdims=True)
    local_of = jnp.max(jnp.where(placed, local[None, :], -1), axis=1, keepdims=True)

    vmem = pl.BlockSpec(memory_space=pltpu.VMEM)
    smem = pl.BlockSpec(memory_space=pltpu.SMEM)
    grid_size = plot_slot.shape[1] * plot_slot.shape[2]
    return pl.pallas_call(
        functools.partial(kernel, n_trial, n_factor, rank_tile),
        out_shape=(
            jax.ShapeDtypeStruct(scores.shape, F32),
            jax.ShapeDtypeStruct(loadings.shape, F32),
        ),
        in_specs=[smem] * 5 + [vmem] * 8,
        out_specs=(vmem, vmem),
        scratch_shapes=[
            pltpu.VMEM((8, rows, PANEL), F32),
            pltpu.VMEM((8, rows, PANEL), F32),
            pltpu.VMEM((2, required, PANEL), F32),
            pltpu.VMEM((2, n_factor, required, PANEL), F32),
            pltpu.VMEM((per_dev, 2 * per_trial, grid_size), BF16),
            pltpu.VMEM((per_dev, PANEL, grid_size), BF16),
            pltpu.VMEM(scores.shape, BF16),
            pltpu.SemaphoreType.DMA((8,)),
            pltpu.SemaphoreType.DMA((8,)),
            pltpu.SemaphoreType.DMA((2, max(n_factor - 1, 1))),
            pltpu.SemaphoreType.DMA((2, max(n_factor - 1, 1))),
        ],
        compiler_params=pltpu.CompilerParams(
            collective_id=0, has_side_effects=True, vmem_limit_bytes=48 * 1024 * 1024
        ),
    )(
        trial_mean,
        correlations,
        noise_var,
        row_count,
        col_count,
        observed,
        plot_slot,
        scores,
        loadings,
        score_precision[:, None],
        source,
        local_of.astype(F32),
        place[:, None],
    )


def solution(mesh):
    in_specs = (
        P("trial", None, None),
        P("trial"),
        P("trial", None),
        P("trial"),
        P("trial", None, None),
        P("trial"),
        P("trial"),
        P("trial", None),
        P("factor", "trial"),
        P("trial", "factor"),
        P("factor"),
    )
    out_specs = (P("factor", "trial"), P("trial", "factor"))
    return jax.shard_map(body, mesh=mesh, in_specs=in_specs, out_specs=out_specs, check_vma=False)
```

time: 441 us -> 56.6 us (0.13)
  the two profiles are of different devices: /device:TPU:14 before, /device:TPU:0 now
where the time goes in v1:
time: 56.6 us; the launch traced here: 56.4 us
  Pallas kernels  50.5 us (89%)
  local copies, waits for them, and re-layouts  4.78 us (8%)
  between operations  0.72 us (1%)
    pallas_call x1, Pallas kernels, body(): pl.pallas_call(functools.partial(kernel, n_trial, n_factor, rank_tile), o...  50.5 us
    unnamed x23, local copies, waits for them, and re-layouts  3.37 us

profile of v1, /device:TPU:0, one launch (start us, length us, event | category | flops | bytes accessed | tf_op | source)
XLA Modules:
  0.0 56.4 jit_solution(93976082281091971)
XLA Ops:
  0.6 0.0 copy-start.8
  0.6 0.0 copy-start
  0.6 0.8 %reshape.127 = s32[64]{0:T(128)S(1)} reshape(s32[4,16]{1,0:T(4,128)} %param.18) | data formatting | bytes 512 | tf_op jit(solution)/shard_map/reshape | solution.py:316
  1.5 0.0 copy-done.8
  1.5 0.2 convert_reduce_fusion
  1.7 0.1 select_reduce_fusion
  1.8 0.8 %copy.34.corr_ref = f32[4,2]{1,0:T(4,128)S(1)} copy(f32[4,2]{0,1:T(2,128)} %param.13) | data formatting | bytes 64 | tf_op args[2]
  2.6 0.1 and.36
  2.7 0.1 div.34
  2.8 0.1 copy.33
  2.9 0.0 copy-start.9
  2.9 0.6 %copy-done.9 = f32[64]{0:T(128)S(1)} copy-done((f32[64]{0:T(128)S(1)}, f32[64]{0:T(128)}, u32[]{:S(2)}) %copy-start.9) | copy-done | bytes 280
  3.5 0.0 copy-start.3
  3.5 0.0 copy-start.6
  3.5 0.0 copy-start.7
  3.5 0.1 copy.35.precision_ref
  3.6 0.0 copy-start.1
  3.6 0.0 copy-start.2
  3.6 0.1 copy.36.source_ref
  3.8 0.0 copy-start.5
  3.8 0.1 copy.37.local_ref
  3.9 0.0 copy-done
  3.9 0.3 copy-done.3
  4.2 0.0 copy-done.6
  4.2 0.0 copy-done.7
  4.2 0.3 copy-done.1
  4.5 0.0 copy-done.2
  4.5 0.0 copy-done.4
  4.5 0.0 copy-done.5
  4.5 50.5 %shard_map.122 = (f32[64,1536]{1,0:T(8,128)S(1)}, f32[4,64]{1,0:T(4,128)S(1)}) custom-call(f32[4]{0:T(128)S(1)} %copy-done.4, f32[4,2]{1,0:T(4,128)S(1)} %copy.34.corr_ref, f32[4]{0:T(128)S(1)} %copy-done.5, s32[4]{0:T(128)S(1)} %copy-done.6, s32[4]{0:T(128)S(1)} %copy-done.7, f32[4,32,128]{2,1,0:T(8,128)S(1)} %copy-done.1, s32[4,32,128]{2,1,0:T(8,128)S(1)} %copy-done.2, ...), custom_call_target="tpu_custom_call" | custom-call | tf_op jit(solution)/shard_map/pallas_call | solution.py:331
  55.0 0.7 %copy.40 = f32[64,1536]{1,0:T(8,128)} copy(f32[64,1536]{1,0:T(8,128)S(1)} %get-tuple-element.8) | data formatting | bytes 786432
  55.8 0.6 %copy.41 = f32[4,64]{1,0:T(4,128)} copy(f32[4,64]{1,0:T(4,128)S(1)} %get-tuple-element.9) | data formatting | bytes 2048
  (7 shorter events, 0.1 us)
Async XLA Ops:
  0.6 0.8 %copy-start.8 = (s32[4,16]{1,0:T(4,128)S(1)}, s32[4,16]{1,0:T(4,128)}, u32[]{:S(2)}) copy-start(s32[4,16]{1,0:T(4,128)} %param.18) | copy-start | bytes 772
  0.6 3.2 %copy-start = (bf16[64,1536]{1,0:T(8,128)(2,1)S(1)}, bf16[64,1536]{1,0:T(8,128)(2,1)}, u32[]{:S(2)}) copy-start(bf16[64,1536]{1,0:T(8,128)(2,1)} %scores_ref.1) | copy-start | bytes 589828
  2.9 0.7 %copy-start.9 = (f32[64]{0:T(128)S(1)}, f32[64]{0:T(128)}, u32[]{:S(2)}) copy-start(f32[64]{0:T(128)} %param.21) | copy-start | bytes 772
  3.5 0.7 %copy-start.3 = (f32[4,64]{1,0:T(4,128)S(1)}, f32[4,64]{1,0:T(4,128)}, u32[]{:S(2)}) copy-start(f32[4,64]{1,0:T(4,128)} %loads_ref.1) | copy-start | bytes 3076
  3.5 0.7 %copy-start.6 = (s32[4]{0:T(128)S(1)}, s32[4]{0:T(128)}, u32[]{:S(2)}) copy-start(s32[4]{0:T(128)} %rows_ref.1) | copy-start | bytes 52
  3.5 0.7 %copy-start.7 = (s32[4]{0:T(128)S(1)}, s32[4]{0:T(128)}, u32[]{:S(2)}) copy-start(s32[4]{0:T(128)} %cols_ref.1) | copy-start | bytes 52
  3.6 0.8 %copy-start.1 = (f32[4,32,128]{2,1,0:T(8,128)S(1)}, f32[4,32,128]{2,1,0:T(8,128)}, u32[]{:S(2)}) copy-start(f32[4,32,128]{2,1,0:T(8,128)} %observed_ref.1) | copy-start | bytes 196612
  3.6 0.9 %copy-start.2 = (s32[4,32,128]{2,1,0:T(8,128)S(1)}, s32[4,32,128]{2,1,0:T(8,128)}, u32[]{:S(2)}) copy-start(s32[4,32,128]{2,1,0:T(8,128)} %slot_ref.1) | copy-start | bytes 196612
  3.8 0.8 %copy-start.4 = (f32[4]{0:T(128)S(1)}, f32[4]{0:T(128)}, u32[]{:S(2)}) copy-start(f32[4]{0:T(128)} %mean_ref.1) | copy-start | bytes 52
  3.8 0.7 %copy-start.5 = (f32[4]{0:T(128)S(1)}, f32[4]{0:T(128)}, u32[]{:S(2)}) copy-start(f32[4]{0:T(128)} %noise_ref.1) | copy-start | bytes 52

commit v2 on v1

v2 whole, which is shorter than its diff:
```python
import functools

import jax
import jax.numpy as jnp
from jax import lax
from jax.experimental import pallas as pl
from jax.experimental.pallas import tpu as pltpu
from jax.sharding import PartitionSpec as P

PANEL = 128
TILE = 8

score_step = 0.005
load_step = 0.02

MESH = pl.DeviceIdType.MESH
F32 = jnp.float32
BF16 = jnp.bfloat16
LEVELS = 32000.0


def halves(x):
    high = x.astype(BF16).astype(F32)
    return high, x - high


def dot(a, b):
    return lax.dot_general(a, b, (((1,), (0,)), ((), ())), preferred_element_type=F32)


def dot_nt(a, b):
    return lax.dot_general(a, b, (((1,), (1,)), ((), ())), preferred_element_type=F32)


def kernel(
    n_trial,
    n_factor,
    rank_tile,
    mean_hbm,
    corr_hbm,
    noise_hbm,
    rows_hbm,
    cols_hbm,
    list_hbm,
    precision_hbm,
    loads_hbm,
    scores_hbm,
    slot_hbm,
    observed_hbm,
    score_out,
    load_out,
    mean_ref,
    corr_ref,
    noise_ref,
    rows_ref,
    cols_ref,
    list_ref,
    precision_ref,
    loads_ref,
    scores_ref,
    slot_ref,
    observed_ref,
    sent,
    got,
    share,
    shares,
    scale,
    scales,
    fac_sent,
    fac_got,
    spread,
    cells,
    fresh,
    copy_sem,
    send_sem,
    recv_sem,
    fac_send_sem,
    fac_recv_sem,
):
    per_dev, grid_rows, grid_cols = observed_ref.shape
    factors = scores_ref.shape[0]
    owned = scores_ref.shape[1] // PANEL
    per_trial = list_ref.shape[1]
    required = per_dev * per_trial
    rows = n_trial * rank_tile
    trials = n_trial * per_dev
    me = lax.axis_index("trial")
    mine = lax.axis_index("factor")

    barrier = pltpu.get_barrier_semaphore()
    for step in range(1, n_trial):
        pl.semaphore_signal(
            barrier,
            inc=1,
            device_id={"trial": lax.rem(me + step, n_trial)},
            device_id_type=MESH,
        )
    for step in range(1, n_factor):
        pl.semaphore_signal(
            barrier,
            inc=1,
            device_id={"factor": lax.rem(mine + step, n_factor)},
            device_id_type=MESH,
        )

    pairs = (
        (list_hbm, list_ref),
        (loads_hbm, loads_ref),
        (slot_hbm, slot_ref),
        (scores_hbm, scores_ref),
        (observed_hbm, observed_ref),
        (precision_hbm, precision_ref),
        (mean_hbm, mean_ref),
        (corr_hbm, corr_ref),
        (noise_hbm, noise_ref),
        (rows_hbm, rows_ref),
        (cols_hbm, cols_ref),
    )
    copies = [
        pltpu.make_async_copy(source, target, copy_sem.at[index])
        for index, (source, target) in enumerate(pairs)
    ]
    for copy in copies:
        copy.start()

    def tile_at(index):
        return pl.ds(pl.multiple_of(index * rank_tile, rank_tile), rank_tile)

    def send(number):
        for step in range(1, n_trial):
            target = lax.rem(me + step, n_trial)
            pltpu.make_async_remote_copy(
                src_ref=sent.at[number, tile_at(target)],
                dst_ref=got.at[number, tile_at(me)],
                send_sem=send_sem.at[number],
                recv_sem=recv_sem.at[number],
                device_id={"trial": target},
                device_id_type=MESH,
            ).start()
        got[number, tile_at(me), :] = sent[number, tile_at(me), :]

    def others(number, ref, sem):
        part = ref.at[number, pl.ds(0, (n_trial - 1) * rank_tile)]
        return pltpu.make_async_copy(part, part, sem.at[number])

    def receive(number):
        others(number, got, recv_sem).wait()
        return got[number]

    def send_share():
        for step in range(1, n_trial):
            pltpu.make_async_remote_copy(
                src_ref=share,
                dst_ref=shares.at[me],
                send_sem=send_sem.at[6],
                recv_sem=recv_sem.at[6],
                device_id={"trial": lax.rem(me + step, n_trial)},
                device_id_type=MESH,
            ).start()
            pltpu.make_async_remote_copy(
                src_ref=scale.at[pl.ds(0, 1)],
                dst_ref=scales.at[pl.ds(me, 1)],
                send_sem=send_sem.at[7],
                recv_sem=recv_sem.at[7],
                device_id={"trial": lax.rem(me + step, n_trial)},
                device_id_type=MESH,
            ).start()
        shares[pl.ds(me, 1)] = share[...][None]
        scales[pl.ds(me, 1), :] = scale[0:1, :]

    def other_shares(sem):
        part = shares.at[pl.ds(0, n_trial - 1)]
        return pltpu.make_async_copy(part, part, sem.at[6])

    def other_scales(sem):
        part = scales.at[pl.ds(0, n_trial - 1)]
        return pltpu.make_async_copy(part, part, sem.at[7])

    def factor_sum(number, part):
        fac_sent[number] = part
        for step in range(1, n_factor):
            pltpu.make_async_remote_copy(
                src_ref=fac_sent.at[number],
                dst_ref=fac_got.at[number, mine],
                send_sem=fac_send_sem.at[number, step - 1],
                recv_sem=fac_recv_sem.at[number, step - 1],
                device_id={"factor": lax.rem(mine + step, n_factor)},
                device_id_type=MESH,
            ).start()
        fac_got[number, pl.ds(mine, 1)] = part[None]
        for step in range(1, n_factor):
            origin = lax.rem(mine + n_factor - step, n_factor)
            pltpu.make_async_copy(
                fac_sent.at[number], fac_got.at[number, origin], fac_recv_sem.at[number, step - 1]
            ).wait()
        total = fac_got[number, 0]
        for index in range(1, n_factor):
            total = total + fac_got[number, index]
        return total

    def column(line):
        size = line.shape[1]
        eye = lax.broadcasted_iota(jnp.int32, (size, size), 0) == lax.broadcasted_iota(
            jnp.int32, (size, size), 1
        )
        return jnp.sum(jnp.where(eye, line, 0.0), axis=1, keepdims=True)

    copies[0].wait()
    wanted = jnp.concatenate(
        [list_ref[trial : trial + 1, :] for trial in range(per_dev)], axis=1
    )
    owner = wanted // owned
    local = wanted - owner * owned
    owner_line = owner.astype(F32)
    before = lax.broadcasted_iota(jnp.int32, (required, required), 0)
    after = lax.broadcasted_iota(jnp.int32, (required, required), 1)
    earlier = (column(owner_line) == owner_line) & (before < after)
    rank = jnp.sum(jnp.where(earlier, 1.0, 0.0), axis=0, keepdims=True)
    place = owner_line * rank_tile + rank
    row_of = lax.broadcasted_iota(jnp.int32, (rows, required), 0).astype(F32)
    placed = place == row_of
    slot_trial = lax.broadcasted_iota(jnp.int32, (rows, required), 1) // per_trial
    trial_of = jnp.max(jnp.where(placed, slot_trial.astype(F32), -1.0), axis=1, keepdims=True)
    local_of = jnp.max(jnp.where(placed, local.astype(F32), -1.0), axis=1, keepdims=True)
    pack = jnp.where(placed, 1.0, 0.0)
    pack = jnp.concatenate([pack, pack], axis=1).astype(BF16)

    copies[1].wait()
    loads = loads_ref[...]
    load_rows = jnp.zeros((rows, factors), F32)
    for trial in range(per_dev):
        load_rows = jnp.where(trial_of == trial, loads[trial : trial + 1, :], load_rows)
    sent[0] = jnp.concatenate(
        [
            load_rows,
            jnp.broadcast_to(local_of, (rows, 8)),
            jnp.broadcast_to(trial_of, (rows, PANEL - factors - 8)),
        ],
        axis=1,
    )
    pl.semaphore_wait(barrier, n_trial - 1 + n_factor - 1)
    send(0)

    lane_rows = lax.broadcasted_iota(jnp.int32, (required, rows), 1).astype(F32)
    unpack = jnp.where(column(place) == lane_rows, 1.0, 0.0).astype(BF16)
    unpack = jnp.concatenate([unpack, unpack], axis=1)
    cell_iota = lax.broadcasted_iota(jnp.int32, (PANEL, grid_cols), 0)
    panel_iota = lax.broadcasted_iota(jnp.int32, (per_trial, grid_cols), 0)
    for copy in copies[2:]:
        copy.wait()
    precision = column(precision_ref[...])
    for trial in range(per_dev):
        cell = slot_ref[trial] & (PANEL - 1)
        for row in range(grid_rows):
            cells[trial, :, row * grid_cols : (row + 1) * grid_cols] = jnp.where(
                cell[row : row + 1, :] == cell_iota, 1.0, 0.0
            ).astype(BF16)

    row_index = lax.broadcasted_iota(jnp.int32, (grid_rows, grid_cols), 0)
    col_index = lax.broadcasted_iota(jnp.int32, (grid_rows, grid_cols), 1)

    def sweep(values, corr, position, limit, axis):
        length = values.shape[axis]
        scale = 1.0 / (1.0 - corr * corr)
        inner = jnp.where((position > 0) & (position < limit - 1), corr * corr, 0.0)
        lower = jnp.where(position == 0, 0.0, pltpu.roll(values, 1, axis))
        upper = jnp.where(position == length - 1, 0.0, pltpu.roll(values, length - 1, axis))
        result = scale * ((1.0 + inner) * values - corr * (lower + upper))
        return jnp.where(position < limit, result, 0.0)

    def over_grid(ref, row, lane):
        return jnp.broadcast_to(ref[row : row + 1, lane : lane + 1], (grid_rows, grid_cols))

    def plots(effect):
        totals = []
        for trial in range(per_dev):
            slot = slot_ref[trial]
            panel = slot // PANEL
            cell = slot & (PANEL - 1)
            fitted = jnp.zeros((grid_rows, grid_cols), F32)
            for index in range(per_trial):
                at = trial * per_trial + index
                line = jnp.broadcast_to(effect[at : at + 1, :], (grid_rows, PANEL))
                taken = jnp.take_along_axis(line, cell, axis=1)
                fitted = jnp.where(panel == index, taken, fitted)
            row_limit = over_grid(rows_ref, 0, trial)
            col_limit = over_grid(cols_ref, 0, trial)
            active = (row_index < row_limit) & (col_index < col_limit)
            residual = jnp.where(
                active, observed_ref[trial] - over_grid(mean_ref, 0, trial) - fitted, 0.0
            )
            across = sweep(residual, over_grid(corr_ref, trial, 1), col_index, col_limit, 1)
            weighted = sweep(across, over_grid(corr_ref, trial, 0), row_index, row_limit, 0)
            weighted = weighted / over_grid(noise_ref, 0, trial)
            high, low = halves(weighted)
            for row in range(grid_rows):
                match = panel[row : row + 1, :] == panel_iota
                where_to = slice(row * grid_cols, (row + 1) * grid_cols)
                spread[trial, 0:per_trial, where_to] = jnp.where(
                    match, high[row : row + 1, :], 0.0
                ).astype(BF16)
                spread[trial, per_trial : 2 * per_trial, where_to] = jnp.where(
                    match, low[row : row + 1, :], 0.0
                ).astype(BF16)
            both = dot_nt(spread[trial], cells[trial])
            totals.append(both[0:per_trial] + both[per_trial : 2 * per_trial])
        return jnp.concatenate(totals, axis=0)

    message = receive(0)
    first_loads = message[:, 0:factors]
    panel_of = message[:, factors : factors + 1]
    turned = message.T
    panel_lane = turned[factors : factors + 1, :]
    block_at = lax.broadcasted_iota(jnp.int32, (rows, 1), 0) // rank_tile * per_dev
    block_lane = lax.broadcasted_iota(jnp.int32, (1, rows), 1) // rank_tile * per_dev
    within = message[:, factors + 8 : factors + 9]
    within_lane = turned[factors + 8 : factors + 9, :]
    whose = jnp.where(within >= 0.0, within + block_at.astype(F32), -1.0)
    whose_lane = jnp.where(within_lane >= 0.0, within_lane + block_lane.astype(F32), -1.0)
    gather = whose == lax.broadcasted_iota(jnp.int32, (rows, trials), 1).astype(F32)
    gather = jnp.where(gather, 1.0, 0.0)
    gather = jnp.concatenate([gather, gather], axis=1).astype(BF16)
    collect = whose_lane == lax.broadcasted_iota(jnp.int32, (trials, rows), 0).astype(F32)
    collect = jnp.where(collect, 1.0, 0.0).astype(BF16)
    collect = jnp.concatenate([collect, collect], axis=1)

    def stacked(values):
        high, low = halves(values)
        return jnp.concatenate([high, low], axis=0).astype(BF16)

    def weigh(number, load_part, current_ref):
        load_high, load_low = halves(load_part)
        load_both = jnp.concatenate([load_high, load_low], axis=1).astype(BF16)
        effect = jnp.zeros((rows, PANEL), F32)
        for panel in range(owned):
            block = current_ref[:, panel * PANEL : (panel + 1) * PANEL]
            product = dot(load_both, jnp.concatenate([block, block], axis=0))
            effect = jnp.where(panel_of == panel, product, effect)
        sent[number] = effect
        send(number)
        table = dot(unpack, stacked(receive(number)))
        slot_weight = plots(factor_sum(0 if number == 1 else 1, table))
        sent[number + 1] = dot(pack, stacked(slot_weight))
        send(number + 1)
        return halves(receive(number + 1))

    def load_terms(high, low, current_ref):
        wide = jnp.concatenate([high, low], axis=1).astype(BF16)
        terms = jnp.zeros((rows, factors), F32)
        for panel in range(owned):
            block = current_ref[:, panel * PANEL : (panel + 1) * PANEL]
            product = dot_nt(wide, jnp.concatenate([block, block], axis=1))
            terms = jnp.where(panel_of == panel, product, terms)
        return terms

    def score_grads(high, low, load_lanes, current_ref):
        tall = jnp.concatenate([high, low, high], axis=0).astype(BF16)
        lane_high, lane_low = halves(load_lanes)
        for panel in range(owned):
            where_to = slice(panel * PANEL, (panel + 1) * PANEL)
            match = panel_lane == panel
            masked_high = jnp.where(match, lane_high, 0.0)
            masked_low = jnp.where(match, lane_low, 0.0)
            left = jnp.concatenate([masked_high, masked_high, masked_low], axis=1).astype(BF16)
            current = current_ref[:, where_to].astype(F32)
            yield where_to, current, precision * current - dot(left, tall)

    padding = jnp.zeros((rows, PANEL - factors), F32)
    high, low = weigh(1, first_loads, scores_ref)
    partial = dot(collect, stacked(load_terms(high, low, scores_ref)))
    groups = PANEL // factors
    depth = trials // groups
    packed = jnp.concatenate(
        [partial[index * depth : (index + 1) * depth] for index in range(groups)], axis=1
    )
    unit = jnp.max(jnp.abs(packed), axis=1, keepdims=True) * (1.0 / LEVELS) + 1e-30
    share[...] = jnp.floor(packed / unit + 0.5).astype(jnp.int32).astype(jnp.int16)
    square = jnp.concatenate(
        [jnp.broadcast_to(unit, (depth, PANEL)), jnp.zeros((PANEL - depth, PANEL), F32)], axis=0
    )
    scale[...] = square.T[0:TILE, :]
    send_share()
    for where_to, current, grad in score_grads(high, low, turned[0:factors, :], scores_ref):
        fresh[:, where_to] = (current - score_step * grad).astype(BF16)
    other_shares(recv_sem).wait()
    other_scales(recv_sem).wait()
    tall_scales = scales[...]
    if n_trial < PANEL:
        tall_scales = jnp.concatenate(
            [tall_scales, jnp.zeros((PANEL - n_trial, PANEL), F32)], axis=0
        )
    units = tall_scales.T[0:depth, :]
    summed = jnp.zeros((depth, PANEL), F32)
    for index in range(n_trial):
        whole = shares[index].astype(jnp.int32).astype(F32)
        summed = summed + whole * units[:, index : index + 1]
    gained = jnp.concatenate(
        [summed[:, index * factors : (index + 1) * factors] for index in range(groups)], axis=0
    )
    second_loads = first_loads + load_step * dot(gather, stacked(gained))
    high, low = weigh(3, second_loads, fresh)
    sent[5] = jnp.concatenate([load_terms(high, low, fresh), padding], axis=1)
    send(5)
    turned_loads = jnp.concatenate([second_loads, padding], axis=1).T[0:factors, :]
    for where_to, current, grad in score_grads(high, low, turned_loads, fresh):
        score_out[:, where_to] = grad
    back = receive(5)[:, 0:factors]
    for trial in range(per_dev):
        load_out[trial : trial + 1, :] = -jnp.sum(
            jnp.where(trial_of == trial, back, 0.0), axis=0, keepdims=True
        )

    for number in range(6):
        others(number, sent, send_sem).wait()
    other_shares(send_sem).wait()
    other_scales(send_sem).wait()
    for number in range(2):
        for step in range(1, n_factor):
            pltpu.make_async_copy(
                fac_sent.at[number], fac_sent.at[number], fac_send_sem.at[number, step - 1]
            ).wait()


def body(
    observed,
    trial_mean,
    correlations,
    noise_var,
    plot_slot,
    row_count,
    col_count,
    panel_list,
    scores,
    loadings,
    score_precision,
):
    n_trial = lax.axis_size("trial")
    n_factor = lax.axis_size("factor")
    per_dev, per_trial = panel_list.shape
    required = per_dev * per_trial
    most = 2 * required // n_trial
    rank_tile = -(-most // TILE) * TILE
    rows = n_trial * rank_tile
    factors = scores.shape[0]
    depth = n_trial * per_dev * factors // PANEL
    grid_size = plot_slot.shape[1] * plot_slot.shape[2]
    operands = (
        trial_mean[None],
        correlations,
        noise_var[None],
        row_count[None],
        col_count[None],
        panel_list,
        score_precision[None],
        loadings,
        scores,
        plot_slot,
        observed,
    )
    vmem = pl.BlockSpec(memory_space=pltpu.VMEM)
    hbm = pl.BlockSpec(memory_space=pltpu.HBM)
    return pl.pallas_call(
        functools.partial(kernel, n_trial, n_factor, rank_tile),
        out_shape=(
            jax.ShapeDtypeStruct(scores.shape, F32),
            jax.ShapeDtypeStruct(loadings.shape, F32),
        ),
        in_specs=[hbm] * len(operands),
        out_specs=(vmem, vmem),
        scratch_shapes=[pltpu.VMEM(operand.shape, operand.dtype) for operand in operands]
        + [
            pltpu.VMEM((6, rows, PANEL), F32),
            pltpu.VMEM((6, rows, PANEL), F32),
            pltpu.VMEM((depth, PANEL), jnp.int16),
            pltpu.VMEM((n_trial, depth, PANEL), jnp.int16),
            pltpu.VMEM((TILE, PANEL), F32),
            pltpu.VMEM((n_trial, PANEL), F32),
            pltpu.VMEM((2, required, PANEL), F32),
            pltpu.VMEM((2, n_factor, required, PANEL), F32),
            pltpu.VMEM((per_dev, 2 * per_trial, grid_size), BF16),
            pltpu.VMEM((per_dev, PANEL, grid_size), BF16),
            pltpu.VMEM(scores.shape, BF16),
            pltpu.SemaphoreType.DMA((len(operands),)),
            pltpu.SemaphoreType.DMA((8,)),
            pltpu.SemaphoreType.DMA((8,)),
            pltpu.SemaphoreType.DMA((2, max(n_factor - 1, 1))),
            pltpu.SemaphoreType.DMA((2, max(n_factor - 1, 1))),
        ],
        compiler_params=pltpu.CompilerParams(
            collective_id=0, has_side_effects=True, vmem_limit_bytes=48 * 1024 * 1024
        ),
    )(*operands)


def solution(mesh):
    in_specs = (
        P("trial", None, None),
        P("trial"),
        P("trial", None),
        P("trial"),
        P("trial", None, None),
        P("trial"),
        P("trial"),
        P("trial", None),
        P("factor", "trial"),
        P("trial", "factor"),
        P("factor"),
    )
    out_specs = (P("factor", "trial"), P("trial", "factor"))
    return jax.shard_map(body, mesh=mesh, in_specs=in_specs, out_specs=out_specs, check_vma=False)
```

time: 56.6 us -> 52.8 us (0.933)
  Pallas kernels: 50.5 us -> 46.6 us
    pallas_call x1, Pallas kernels: 50.5 us -> 46.6 us  [body(): pl.pallas_call(functools.partial(kernel, n_trial, n_factor, rank_tile), o...]
    unnamed x23 -> x25, local copies, waits for them, and re-layouts: 3.37 us -> 5.19 us
    reshape x1 -> x0, local copies, waits for them, and re-layouts: 0.82 us -> none  [body(): wanted = panel_list.reshape(required)]
where the time goes in v2:
time: 52.8 us; the launch traced here: 52.5 us
  Pallas kernels  46.6 us (88%)
  local copies, waits for them, and re-layouts  5.19 us (10%)
  between operations  0.73 us (1%)
    pallas_call x1, Pallas kernels, body(): pl.pallas_call(functools.partial(kernel, n_trial, n_factor, rank_tile), o...  46.6 us
    unnamed x25, local copies, waits for them, and re-layouts  5.19 us

profile of v2, /device:TPU:0, one launch (start us, length us, event | category | flops | bytes accessed | tf_op | source)
XLA Modules:
  0.0 52.5 jit_solution(9264889273003542116)
XLA Ops:
  0.6 0.0 copy-start.10
  0.6 0.0 copy-start.6
  0.7 0.0 copy-start.7
  0.7 0.0 copy-start.8
  0.7 0.0 copy-start.9
  0.7 0.0 copy-start.3
  0.7 0.0 copy-start.4
  0.7 0.6 %copy-done.10 = f32[4,2]{0,1:T(2,128)S(1)} copy-done((f32[4,2]{0,1:T(2,128)S(1)}, f32[4,2]{0,1:T(2,128)}, u32[]{:S(2)}) %copy-start.10) | copy-done | bytes 56
  1.3 0.0 copy-start.5
  1.3 0.1 copy.13.corr_hbm
  1.4 0.0 copy-done.6
  1.4 0.0 copy-done.7
  1.4 0.0 copy-done.8
  1.4 0.0 copy-done.9
  1.4 0.0 copy-done.3
  1.4 0.0 copy-done.4
  1.4 0.5 copy-done.5
  2.0 0.0 copy-start
  2.0 0.9 %copy-done = bf16[64,1536]{1,0:T(8,128)(2,1)S(1)} copy-done((bf16[64,1536]{1,0:T(8,128)(2,1)S(1)}, bf16[64,1536]{1,0:T(8,128)(2,1)}, u32[]{:S(2)}) %copy-start) | copy-done | bytes 196632
  2.9 0.0 copy-start.1
  2.9 0.8 %copy-done.1 = s32[4,32,128]{2,1,0:T(8,128)S(1)} copy-done((s32[4,32,128]{2,1,0:T(8,128)S(1)}, s32[4,32,128]{2,1,0:T(8,128)}, u32[]{:S(2)}) %copy-start.1) | copy-done | bytes 65560
  3.7 0.0 copy-start.2
  3.7 0.8 %copy-done.2 = f32[4,32,128]{2,1,0:T(8,128)S(1)} copy-done((f32[4,32,128]{2,1,0:T(8,128)S(1)}, f32[4,32,128]{2,1,0:T(8,128)}, u32[]{:S(2)}) %copy-start.2) | copy-done | bytes 65560
  4.6 46.6 %shard_map.122 = (f32[64,1536]{1,0:T(8,128)S(1)}, f32[4,64]{1,0:T(4,128)S(1)}) custom-call(f32[1,4]{1,0:T(1,128)S(1)} %bitcast.5, f32[4,2]{1,0:T(4,128)S(1)} %copy.13.corr_hbm, f32[1,4]{1,0:T(1,128)S(1)} %bitcast.6, s32[1,4]{1,0:T(1,128)S(1)} %bitcast.7, s32[1,4]{1,0:T(1,128)S(1)} %bitcast.8, s32[4,16]{1,0:T(4,128)S(1)} %copy-done.3, f32[1,64]{1,0:T(1,128)S(1)} %bitcast.9, ...), custom_call_target="tpu_custom_call" | custom-call | tf_op jit(solution)/shard_map/pallas_call | solution.py:462
  51.2 0.7 %copy.16 = f32[64,1536]{1,0:T(8,128)} copy(f32[64,1536]{1,0:T(8,128)S(1)} %get-tuple-element.4) | data formatting | bytes 786432
  52.0 0.6 %copy.17 = f32[4,64]{1,0:T(4,128)} copy(f32[4,64]{1,0:T(4,128)S(1)} %get-tuple-element.5) | data formatting | bytes 2048
Async XLA Ops:
  0.6 0.7 %copy-start.10 = (f32[4,2]{0,1:T(2,128)S(1)}, f32[4,2]{0,1:T(2,128)}, u32[]{:S(2)}) copy-start(f32[4,2]{0,1:T(2,128)} %param.13) | copy-start | bytes 100
  0.6 0.8 %copy-start.6 = (f32[4]{0:T(128)S(1)}, f32[4]{0:T(128)}, u32[]{:S(2)}) copy-start(f32[4]{0:T(128)} %param.14) | copy-start | bytes 52
  0.7 0.8 %copy-start.7 = (s32[4]{0:T(128)S(1)}, s32[4]{0:T(128)}, u32[]{:S(2)}) copy-start(s32[4]{0:T(128)} %param.16) | copy-start | bytes 52
  0.7 0.8 %copy-start.8 = (s32[4]{0:T(128)S(1)}, s32[4]{0:T(128)}, u32[]{:S(2)}) copy-start(s32[4]{0:T(128)} %param.17) | copy-start | bytes 52
  0.7 0.7 %copy-start.9 = (f32[64]{0:T(128)S(1)}, f32[64]{0:T(128)}, u32[]{:S(2)}) copy-start(f32[64]{0:T(128)} %param.21) | copy-start | bytes 772
  0.7 0.7 %copy-start.3 = (s32[4,16]{1,0:T(4,128)S(1)}, s32[4,16]{1,0:T(4,128)}, u32[]{:S(2)}) copy-start(s32[4,16]{1,0:T(4,128)} %list_hbm.1) | copy-start | bytes 772
  0.7 0.7 %copy-start.4 = (f32[4,64]{1,0:T(4,128)S(1)}, f32[4,64]{1,0:T(4,128)}, u32[]{:S(2)}) copy-start(f32[4,64]{1,0:T(4,128)} %loads_hbm.1) | copy-start | bytes 3076
  1.3 0.7 %copy-start.5 = (f32[4]{0:T(128)S(1)}, f32[4]{0:T(128)}, u32[]{:S(2)}) copy-start(f32[4]{0:T(128)} %param.12) | copy-start | bytes 52
  2.0 0.9 %copy-start = (bf16[64,1536]{1,0:T(8,128)(2,1)S(1)}, bf16[64,1536]{1,0:T(8,128)(2,1)}, u32[]{:S(2)}) copy-start(bf16[64,1536]{1,0:T(8,128)(2,1)} %scores_hbm.1) | copy-start | bytes 589828
  2.9 0.8 %copy-start.1 = (s32[4,32,128]{2,1,0:T(8,128)S(1)}, s32[4,32,128]{2,1,0:T(8,128)}, u32[]{:S(2)}) copy-start(s32[4,32,128]{2,1,0:T(8,128)} %slot_hbm.1) | copy-start | bytes 196612
  3.7 0.8 %copy-start.2 = (f32[4,32,128]{2,1,0:T(8,128)S(1)}, f32[4,32,128]{2,1,0:T(8,128)}, u32[]{:S(2)}) copy-start(f32[4,32,128]{2,1,0:T(8,128)} %observed_hbm.1) | copy-start | bytes 196612
